TPU v7x, 256 devices: a whole 4x4x8 slice. The times are simulated.
256 devices in a mesh: stream: 16 (over y, z_hi, core), span: 16 (over z_lo, x).
Axes of the slice: x: 4, y: 4, z: 8 (z_hi: 2, z_lo: 4; z = z_hi * 4 + z_lo), core: 2. Of those that a mesh axis runs over, the one named last changes fastest.
Arguments:
- velocity_modes: bfloat16 [32, 128, 10, 3, 128], P('stream', 'span'), may hold values from -6 to 6
- cell_weight: float32 [32, 128, 10], P('stream', 'span'), may hold values from 0.001 to 0.01
Outputs:
- convection: float32 [128, 128, 128], replicated
All inputs are finite; a program needn't handle non-finite values.
Results may differ from a plain program's by a relative error of at most 0.0085.
Values may be sent and summed in bfloat16 or wider, within the bound.
A program may use at most 64 MiB of HBM per device.

v0:
```python
import jax
import jax.numpy as jnp
from jax import lax
from jax.sharding import PartitionSpec as P


def with_halo(cells, sides, width):
    for axis, dim in sides:
        count = lax.axis_size(axis)
        ends = count - 1
        head = lax.slice_in_dim(cells, 0, width, axis=dim)
        tail = lax.slice_in_dim(cells, cells.shape[dim] - width, cells.shape[dim], axis=dim)
        cells = jnp.concatenate(
            [
                lax.ppermute(tail, axis, [(i, (i + 1) % count) for i in range(ends)]),
                cells,
                lax.ppermute(head, axis, [((i + 1) % count, i) for i in range(ends)]),
            ],
            axis=dim,
        )
    return cells


def gradient(padded):
    core_x = padded[:, 2:-2]
    deriv_x = (8.0 * (core_x[3:-1] - core_x[1:-3]) - (core_x[4:] - core_x[:-4])) / 12.0
    core_y = padded[2:-2]
    deriv_y = (8.0 * (core_y[:, 3:-1] - core_y[:, 1:-3]) - (core_y[:, 4:] - core_y[:, :-4])) / 12.0
    center = padded[2:-2, 2:-2]
    vertical = jnp.pad(center, ((0, 0), (0, 0), (1, 1), (0, 0), (0, 0)))
    deriv_z = 0.5 * (vertical[:, :, 2:] - vertical[:, :, :-2])
    return jnp.stack([deriv_x, deriv_y, deriv_z])


def shards(velocity_modes, cell_weight):
    padded = with_halo(velocity_modes, (("stream", 0), ("span", 1)), 2)
    grads = gradient(padded.astype(jnp.float32))
    width = velocity_modes.shape[-1]
    cells = velocity_modes.shape[0] * velocity_modes.shape[1] * velocity_modes.shape[2]
    phi_half = velocity_modes.reshape(cells, 3, width)
    grad_cells = grads.reshape(3, cells, 3, width)
    grad_high = grad_cells.astype(jnp.bfloat16)
    grad_low = (grad_cells - grad_high.astype(jnp.float32)).astype(jnp.bfloat16)
    weight_cells = cell_weight.reshape(cells)
    test_count = width * width // width
    block_size = min(8, test_count)
    turns = test_count // block_size

    def one_block(turn_index, result):
        test_start = turn_index * block_size
        phi_test = lax.dynamic_slice_in_dim(phi_half, test_start, block_size, 2)
        quad = jnp.einsum("cbi,acbk->acik", phi_test, grad_high, preferred_element_type=jnp.float32)
        quad = quad + jnp.einsum(
            "cbi,acbk->acik", phi_test, grad_low, preferred_element_type=jnp.float32
        )
        quad = (quad * weight_cells[None, :, None, None]).astype(jnp.bfloat16)
        block_terms = jnp.einsum(
            "caj,acik->ijk", phi_half, quad, preferred_element_type=jnp.float32
        )
        return lax.dynamic_update_slice_in_dim(
            result, block_terms, (turn_index * block_size).astype(jnp.int32), 0
        )

    result = jnp.zeros((test_count, width, width), jnp.float32)
    result = lax.fori_loop(0, turns, one_block, result)
    whole = lax.psum(result.reshape(test_count * width, width), ("stream", "span"))
    return whole.reshape(width, width, width)


def solution(mesh):
    placed = (P("stream", "span", None, None, None), P("stream", "span", None))
    return jax.shard_map(shards, mesh=mesh, in_specs=placed, out_specs=P(), check_vma=False)
```

profile of v0, /device:TPU:97, one launch (start us, length us, event | category | flops | bytes accessed | tf_op | source)
XLA Modules:
  0.0 390.1 jit_solution(13698949483575971565)
XLA Ops:
  6.5 6.7 %collective-permute-start = (bf16[2,8,10,3,128]{4,1,3,2,0:T(8,128)(2,1)}, bf16[2,8,10,3,128]{4,1,3,2,0:T(8,128)(2,1)S(1)}, u32[]{:S(2)}, u32[]{:S(2)}) collective-permute-start(bf16[2,8,10,3,128]{4,1,3,2,0:T(8,128)(2,1)} %param.4), channel_id=1, source_target_pairs={{0,16},{16,32},{32,48},{48,64},{64,80},{80,96},{96,112},{112,128},... | collective-permute-start | bytes 368648 | tf_op jit(solution)/shard_map/ppermute | solution.py:15
  13.2 1.9 collective-permute-start.1
  15.1 0.7 collective-permute-done
  15.9 0.9 constant_dynamic-update-slice_fusion.2
  16.8 6.9 %collective-permute-done.1 = bf16[2,8,10,3,128]{4,1,3,2,0:T(8,128)(2,1)S(1)} collective-permute-done((bf16[2,8,10,3,128]{4,1,3,2,0:T(8,128)(2,1)}, bf16[2,8,10,3,128]{4,1,3,2,0:T(8,128)(2,1)S(1)}, u32[]{:S(2)}, u32[]{:S(2)}) %collective-permute-start.1) | collective-permute-done | bytes 122912 | tf_op jit(solution)/shard_map/ppermute | solution.py:17
  23.8 3.1 collective-permute-start.2
  26.9 4.8 %collective-permute-start.3 = (bf16[6,2,10,3,128]{4,1,3,2,0:T(2,128)(2,1)S(1)}, bf16[6,2,10,3,128]{4,1,3,2,0:T(2,128)(2,1)S(1)}, u32[]{:S(2)}, u32[]{:S(2)}) collective-permute-start(bf16[6,2,10,3,128]{4,1,3,2,0:T(2,128)(2,1)S(1)} %get-tuple-element.131), channel_id=1, source_target_pairs={{1,0},{2,1},{3,2},{4,3},{5,4},{6,5},{7,6},{8,7},{9,8},{10,9},{11,1... | collective-permute-start | bytes 276488 | tf_op jit(solution)/shard_map/ppermute | solution.py:17
  31.8 0.9 copy.8
  32.7 0.8 mul.67
  35.0 4.5 %broadcast_in_dim.3.clone = f32[128,128,128]{2,1,0:T(8,128)} broadcast(f32[]{:T(128)} %constant.37.clone.1), dimensions={} | broadcast | bytes 8388612 | tf_op jit(solution)/shard_map/broadcast_in_dim | solution.py:64
  39.5 55.6 %while.14 = (s32[]{:T(128)}, f32[128,128,128]{2,1,0:T(8,128)}, bf16[160,3,128]{2,0,1:T(8,128)(2,1)S(1)}, bf16[3,160,3,128]{3,2,1,0:T(4,128)(2,1)S(1)}, bf16[3,16...) while((s32[]{:T(128)}, f32[128,128,128]{2,1,0:T(8,128)}, ...), condition=%wide.wide.region_1.2_spmd, body=%wide.wide.region_0.1_spmd.sunk | while | flops 133201928 | bytes 11377443 | solution.py:65
  40.2 0.6 fusion.44
  40.7 1.2 convolution_bitcast_fusion.3
  42.1 0.8 constant_dynamic-update-slice_fusion.6
  44.2 1.2 convolution_bitcast_fusion.3
  45.6 0.8 constant_dynamic-update-slice_fusion.6
  47.7 1.2 convolution_bitcast_fusion.3
  49.1 0.8 constant_dynamic-update-slice_fusion.6
  50.0 0.6 fusion.45
  51.2 1.2 convolution_bitcast_fusion.3
  52.5 0.8 constant_dynamic-update-slice_fusion.6
  54.6 1.2 convolution_bitcast_fusion.3
  56.0 0.8 constant_dynamic-update-slice_fusion.6
  58.1 1.2 convolution_bitcast_fusion.3
  59.5 0.8 constant_dynamic-update-slice_fusion.6
  61.6 1.2 convolution_bitcast_fusion.3
  62.9 0.8 constant_dynamic-update-slice_fusion.6
  65.1 1.2 convolution_bitcast_fusion.3
  66.4 0.8 constant_dynamic-update-slice_fusion.6
  68.5 1.2 convolution_bitcast_fusion.3
  69.9 0.8 constant_dynamic-update-slice_fusion.6
  72.0 1.2 convolution_bitcast_fusion.3
  73.4 0.8 constant_dynamic-update-slice_fusion.6
  75.5 1.2 convolution_bitcast_fusion.3
  76.8 0.8 constant_dynamic-update-slice_fusion.6
  78.9 1.2 convolution_bitcast_fusion.3
  80.3 0.8 constant_dynamic-update-slice_fusion.6
  82.4 1.2 convolution_bitcast_fusion.3
  83.8 0.8 constant_dynamic-update-slice_fusion.6
  85.9 1.2 convolution_bitcast_fusion.3
  87.2 0.8 constant_dynamic-update-slice_fusion.6
  89.4 1.2 convolution_bitcast_fusion.3
  90.7 0.8 constant_dynamic-update-slice_fusion.6
  91.7 0.6 fusion.45
  92.8 1.2 convolution_bitcast_fusion.3
  94.2 0.8 constant_dynamic-update-slice_fusion.6
  95.1 280.3 %all-reduce.3.cloned.1.call-done = f32[128,128,128]{2,1,0:T(8,128)} async-done(((f32[128,128,128]{2,1,0:T(8,128)}), f32[128,128,128]{2,1,0:T(8,128)}) %all-reduce.3.cloned.1.call-update) | async-done | bytes 8388624 | tf_op jit(solution)/shard_map/psum | solution.py:66
  375.4 7.9 %copy.73 = f32[128,128,128]{2,1,0:T(8,128)} copy(f32[128,128,128]{2,1,0:T(8,128)} %all-reduce.3.cloned.1.call-done) | data formatting | bytes 16777216
  (77 shorter events, 23.1 us)
Async XLA Ops:
  6.5 368.8 %all-reduce.3.cloned.1.call-start = ((), (), s32[]{:S(2)}) async-start(), calls=%async_computation | async-start | bytes 16777216 | tf_op jit(solution)/shard_map/psum | solution.py:66
  6.5 9.3 %collective-permute-start = (bf16[2,8,10,3,128]{4,1,3,2,0:T(8,128)(2,1)}, bf16[2,8,10,3,128]{4,1,3,2,0:T(8,128)(2,1)S(1)}, u32[]{:S(2)}, u32[]{:S(2)}) collective-permute-start(bf16[2,8,10,3,128]{4,1,3,2,0:T(8,128)(2,1)} %param.4), channel_id=1, source_target_pairs={{0,16},{16,32},{32,48},{48,64},{64,80},{80,96},{96,112},{112,128},... | collective-permute-start | bytes 368648 | tf_op jit(solution)/shard_map/ppermute | solution.py:15
  13.2 10.4 %collective-permute-start.1 = (bf16[2,8,10,3,128]{4,1,3,2,0:T(8,128)(2,1)}, bf16[2,8,10,3,128]{4,1,3,2,0:T(8,128)(2,1)S(1)}, u32[]{:S(2)}, u32[]{:S(2)}) collective-permute-start(bf16[2,8,10,3,128]{4,1,3,2,0:T(8,128)(2,1)} %param.4), channel_id=1, source_target_pairs={{16,0},{32,16},{48,32},{64,48},{80,64},{96,80},{112,96},{128,112},... | collective-permute-start | bytes 368648 | tf_op jit(solution)/shard_map/ppermute | solution.py:17
  23.8 9.8 %collective-permute-start.2 = (bf16[6,2,10,3,128]{4,1,3,2,0:T(2,128)(2,1)S(1)}, bf16[6,2,10,3,128]{4,1,3,2,0:T(2,128)(2,1)S(1)}, u32[]{:S(2)}, u32[]{:S(2)}) collective-permute-start(bf16[6,2,10,3,128]{4,1,3,2,0:T(2,128)(2,1)S(1)} %get-tuple-element.130), channel_id=1, source_target_pairs={{0,1},{1,2},{2,3},{3,4},{4,5},{5,6},{6,7},{7,8},{8,9},{9,10},{10,1... | collective-permute-start | bytes 276488 | tf_op jit(solution)/shard_map/ppermute | solution.py:15
  26.9 6.7 %collective-permute-start.3 = (bf16[6,2,10,3,128]{4,1,3,2,0:T(2,128)(2,1)S(1)}, bf16[6,2,10,3,128]{4,1,3,2,0:T(2,128)(2,1)S(1)}, u32[]{:S(2)}, u32[]{:S(2)}) collective-permute-start(bf16[6,2,10,3,128]{4,1,3,2,0:T(2,128)(2,1)S(1)} %get-tuple-element.131), channel_id=1, source_target_pairs={{1,0},{2,1},{3,2},{4,3},{5,4},{6,5},{7,6},{8,7},{9,8},{10,9},{11,1... | collective-permute-start | bytes 276488 | tf_op jit(solution)/shard_map/ppermute | solution.py:17
Sparse Core Ops, SparseCore 0:
  95.2 280.1 all-reduce.2
where the time goes:
time: 390 us
  waiting for transfers between devices  288 us (74%)
  matrix products  36.9 us (9%)
  local copies, waits for them, and re-layouts  33.7 us (9%)
  starting transfers between devices  16.6 us (4%)
  between operations  13.5 us (3%)
    psum x1, waiting for transfers between devices, shards(): lax.psum(result.reshape(test_count * width, width), ('stream', 'span'))  280 us
    dot_general x16, matrix products, one_block(): jnp.einsum('caj,acik->ijk', phi_half, quad, preferred_element_type=jnp.fl...  18.4 us
    dynamic_update_slice x32, local copies, waits for them, and re-layouts, one_block(): lax.dynamic_update_slice_in_dim(result, block_terms, (turn_index * block_...  16.6 us
    ppermute x2, starting transfers between devices, with_halo(): lax.ppermute(tail, axis, [(i, (i + 1) % count) for i in range(ends)])  9.79 us
    unnamed x4, local copies, waits for them, and re-layouts  9.77 us
    dot_general x16, matrix products, one_block(): jnp.einsum('cbi,acbk->acik', phi_test, grad_high, preferred_element_type=...  9.23 us
    dot_general x16, matrix products, one_block(): jnp.einsum('cbi,acbk->acik', phi_test, grad_low, preferred_element_type=j...  9.22 us
  transfers between devices with their start and end apart: 5, of which 3 were waited for; matrix products, arithmetic and copies ran while one was open for 1% of the time, Pallas kernels for 0%

commit v1 on v0

--- a/solution.py
+++ b/solution.py
@@ -63,7 +63,7 @@
 
     result = jnp.zeros((test_count, width, width), jnp.float32)
     result = lax.fori_loop(0, turns, one_block, result)
-    whole = lax.psum(result.reshape(test_count * width, width), ("stream", "span"))
+    whole = lax.psum(lax.psum(result.reshape(test_count * width, width), "span"), "stream")
     return whole.reshape(width, width, width)
 
 

time: 390 us -> 699 us (1.79)
  the two profiles are of different devices: /device:TPU:97 before, /device:TPU:2 now
where the time goes in v1:
time: 699 us
  waiting for transfers between devices  604 us (86%)
  matrix products  36.9 us (5%)
  local copies, waits for them, and re-layouts  33.7 us (5%)
  between operations  13.5 us (2%)
  starting transfers between devices  8.92 us (1%)
    psum x1, waiting for transfers between devices, shards(): lax.psum(lax.psum(result.reshape(test_count * width, width), 'span'), 'st...  383 us
    psum x1, waiting for transfers between devices, shards(): lax.psum(result.reshape(test_count * width, width), 'span')  211 us
    dot_general x16, matrix products, one_block(): jnp.einsum('caj,acik->ijk', phi_half, quad, preferred_element_type=jnp.fl...  18.4 us
    dynamic_update_slice x32, local copies, waits for them, and re-layouts, one_block(): lax.dynamic_update_slice_in_dim(result, block_terms, (turn_index * block_...  16.6 us
  transfers between devices with their start and end apart: 6, of which 4 were waited for; matrix products, arithmetic and copies ran while one was open for 0% of the time, Pallas kernels for 0%

profile of v1, /device:TPU:2, one launch (start us, length us, event | category | flops | bytes accessed | tf_op | source)
XLA Modules:
  0.0 699.0 jit_solution(6642513552538497321)
XLA Ops:
  6.5 1.7 collective-permute-start
  8.3 1.3 collective-permute-start.1
  9.6 0.9 constant_dynamic-update-slice_fusion.2
  10.5 8.2 %collective-permute-done.1 = bf16[2,8,10,3,128]{4,1,3,2,0:T(8,128)(2,1)S(1)} collective-permute-done((bf16[2,8,10,3,128]{4,1,3,2,0:T(8,128)(2,1)}, bf16[2,8,10,3,128]{4,1,3,2,0:T(8,128)(2,1)S(1)}, u32[]{:S(2)}, u32[]{:S(2)}) %collective-permute-start.1) | collective-permute-done | bytes 122912 | tf_op jit(solution)/shard_map/ppermute | solution.py:17
  18.8 3.4 collective-permute-start.2
  22.3 2.4 collective-permute-start.3
  24.7 0.9 copy.7
  25.7 0.8 mul.67
  26.5 2.2 collective-permute-done.3
  30.1 4.5 broadcast_in_dim.3.clone
  34.6 55.6 %while.14 = (s32[]{:T(128)}, f32[128,128,128]{2,1,0:T(8,128)}, bf16[160,3,128]{2,0,1:T(8,128)(2,1)S(1)}, bf16[3,160,3,128]{3,2,1,0:T(4,128)(2,1)S(1)}, bf16[3,16...) while((s32[]{:T(128)}, f32[128,128,128]{2,1,0:T(8,128)}, ...), condition=%wide.wide.region_1.2_spmd, body=%wide.wide.region_0.1_spmd.sunk | while | flops 133201928 | bytes 11377443 | solution.py:65
  35.9 1.2 convolution_bitcast_fusion.3
  37.2 0.8 constant_dynamic-update-slice_fusion.6
  39.3 1.2 convolution_bitcast_fusion.3
  40.7 0.8 constant_dynamic-update-slice_fusion.6
  42.8 1.2 convolution_bitcast_fusion.3
  44.2 0.8 constant_dynamic-update-slice_fusion.6
  45.1 0.6 fusion.45
  46.3 1.2 convolution_bitcast_fusion.3
  47.6 0.8 constant_dynamic-update-slice_fusion.6
  49.7 1.2 convolution_bitcast_fusion.3
  51.1 0.8 constant_dynamic-update-slice_fusion.6
  53.2 1.2 convolution_bitcast_fusion.3
  54.6 0.8 constant_dynamic-update-slice_fusion.6
  55.5 0.6 fusion.45
  56.7 1.2 convolution_bitcast_fusion.3
  58.1 0.8 constant_dynamic-update-slice_fusion.6
  60.2 1.2 convolution_bitcast_fusion.3
  61.5 0.8 constant_dynamic-update-slice_fusion.6
  63.6 1.2 convolution_bitcast_fusion.3
  65.0 0.8 constant_dynamic-update-slice_fusion.6
  67.1 1.2 convolution_bitcast_fusion.3
  68.5 0.8 constant_dynamic-update-slice_fusion.6
  70.6 1.2 convolution_bitcast_fusion.3
  71.9 0.8 constant_dynamic-update-slice_fusion.6
  74.1 1.2 convolution_bitcast_fusion.3
  75.4 0.8 constant_dynamic-update-slice_fusion.6
  77.5 1.2 convolution_bitcast_fusion.3
  78.9 0.8 constant_dynamic-update-slice_fusion.6
  81.0 1.2 convolution_bitcast_fusion.3
  82.4 0.8 constant_dynamic-update-slice_fusion.6
  84.5 1.2 convolution_bitcast_fusion.3
  85.8 0.8 constant_dynamic-update-slice_fusion.6
  87.9 1.2 convolution_bitcast_fusion.3
  89.3 0.8 constant_dynamic-update-slice_fusion.6
  90.2 210.8 %all-reduce.4.cloned.1.call-done = f32[16384,128]{1,0:T(8,128)} async-done(((f32[16384,128]{1,0:T(8,128)}), f32[16384,128]{1,0:T(8,128)}) %all-reduce.4.cloned.1.call-update) | async-done | bytes 8388624 | tf_op jit(solution)/shard_map/psum | solution.py:66
  301.0 383.2 %all-reduce.6.cloned.1.call-done = f32[128,128,128]{2,1,0:T(8,128)} async-done(((f32[128,128,128]{2,1,0:T(8,128)}), f32[128,128,128]{2,1,0:T(8,128)}) %all-reduce.6.cloned.1.call-update) | async-done | bytes 8388624 | tf_op jit(solution)/shard_map/psum | solution.py:66
  684.3 7.9 %copy.73 = f32[128,128,128]{2,1,0:T(8,128)} copy(f32[128,128,128]{2,1,0:T(8,128)} %all-reduce.6.cloned.1.call-done) | data formatting | bytes 16777216
  (80 shorter events, 23.8 us)
Async XLA Ops:
  6.5 294.5 %all-reduce.4.cloned.1.call-start = ((), (), s32[]{:S(2)}) async-start(), calls=%async_computation | async-start | bytes 16777216 | tf_op jit(solution)/shard_map/psum | solution.py:66
  6.5 3.0 collective-permute-start
  8.3 10.4 %collective-permute-start.1 = (bf16[2,8,10,3,128]{4,1,3,2,0:T(8,128)(2,1)}, bf16[2,8,10,3,128]{4,1,3,2,0:T(8,128)(2,1)S(1)}, u32[]{:S(2)}, u32[]{:S(2)}) collective-permute-start(bf16[2,8,10,3,128]{4,1,3,2,0:T(8,128)(2,1)} %param.4), channel_id=1, source_target_pairs={{16,0},{32,16},{48,32},{64,48},{80,64},{96,80},{112,96},{128,112},... | collective-permute-start | bytes 368648 | tf_op jit(solution)/shard_map/ppermute | solution.py:17
  18.8 7.6 %collective-permute-start.2 = (bf16[6,2,10,3,128]{4,1,3,2,0:T(2,128)(2,1)S(1)}, bf16[6,2,10,3,128]{4,1,3,2,0:T(2,128)(2,1)S(1)}, u32[]{:S(2)}, u32[]{:S(2)}) collective-permute-start(bf16[6,2,10,3,128]{4,1,3,2,0:T(2,128)(2,1)S(1)} %get-tuple-element.130), channel_id=1, source_target_pairs={{0,1},{1,2},{2,3},{3,4},{4,5},{5,6},{6,7},{7,8},{8,9},{9,10},{10,1... | collective-permute-start | bytes 276488 | tf_op jit(solution)/shard_map/ppermute | solution.py:15
  22.3 6.4 collective-permute-start.3
  90.2 594.1 %all-reduce.6.cloned.1.call-start = ((), (), s32[]{:S(2)}) async-start(), calls=%async_computation.1 | async-start | bytes 16777216 | tf_op jit(solution)/shard_map/psum | solution.py:66
Sparse Core Ops, SparseCore 0:
  90.3 210.6 all-reduce.3
  303.7 380.5 all-reduce.5
